TPU v7x, 32 devices: a whole 2x2x4 slice. The times are simulated.
32 devices in a mesh: grp: 8 (over z, x), mem: 4 (over y, core).
Axes of the slice: x: 2, y: 2, z: 4, core: 2. Of those that a mesh axis runs over, the one named last changes fastest.
Arguments:
- right_side: float32 [32, 65536], P(None, ('grp', 'mem')), may hold values from -6 to 6
- fine_tiles: float32 [512, 3, 128, 128], P(('grp', 'mem')), may hold values from -0.13492627 to 6.130239
- fine_columns: int32 [512, 3], P(('grp', 'mem')), may hold values from 0 to 19, as said below
- fine_sends: int32 [64, 256], P(('grp', 'mem')), may hold values from 0 to 2047, as said below
- fine_weights: float32 [65536], P(('grp', 'mem')), may hold values from 0.5 to 2
- fine_groups: int32 [65536], P(('grp', 'mem')), may hold values from 0 to 255, as said below
- group_tiles: float32 [64, 3, 128, 128], P('grp'), may hold values from -1.0794102 to 49.0419102
- group_columns: int32 [64, 3], P('grp'), may hold values from 0 to 9, as said below
- group_sends: int32 [16, 128], P('grp'), may hold values from 0 to 1023, as said below
- group_weights: float32 [8192], P('grp'), may hold values from 0.5 to 2
- group_groups: int32 [8192], P('grp'), may hold values from 0 to 31, as said below
- coarse_tiles: float32 [2, 3, 128, 128], replicated, may hold values from -2.1588203 to 98.08382034355964
- coarse_columns: int32 [2, 3], replicated, may hold values from 0 to 1, as said below
Outputs:
- solution: float32 [32, 65536], P(None, ('grp', 'mem'))
- residual: float32 [32, 65536], P(None, ('grp', 'mem'))
Inputs may be any that keep to these rules, and one draw needn't show every extreme that they name: `fine_columns`: fine tiles: within each owner's 16 tile rows, entry 0 is the tile row's own index; entries 1 each name a distinct block of the extended vector (16 own blocks, then 2 from the lower neighbour, then 2 from the higher), and so do entries 2; every halo block is named by entries 2. `fine_sends`: each list holds 256 distinct rows of its owner; list 2 o goes to owner o - 1, list 2 o + 1 to owner o + 1. `fine_groups`: each aggregate of an owner takes exactly 8 of its rows. `group_columns`: as for fine_columns, per group, with 8 tile rows and 2 halo blocks. `group_sends`: each list holds 128 distinct rows of its group. `group_groups`: each aggregate of a group takes exactly 32 of its rows. `coarse_columns`: entry 0 is the tile row's own index; entries 1 name each block once, and so do entries 2.
All inputs are finite; a program needn't handle non-finite values.
Results may differ from a plain program's by a relative error of at most 0.0003.
Values sent between devices are 32-bit elements; how exact they have to be, the bound alone decides.
A program may use at most 128 MiB of HBM per device.

v0:
```python
import functools

import jax
import jax.numpy as jnp
from jax import lax
from jax.experimental import pallas as pl
from jax.experimental.pallas import tpu as pltpu
from jax.sharding import PartitionSpec as P

ITERS = 2
RELAXATION = 0.7
AGG1 = 8
AGG2 = 32
F32, BF16 = jnp.float32, jnp.bfloat16
MESH = pl.DeviceIdType.MESH


def high_part(x):
    return x.astype(BF16)


def low_part(x):
    return (x - x.astype(BF16).astype(F32)).astype(BF16)


def split(x):
    return jnp.concatenate([high_part(x), low_part(x)], axis=0)


def joined(y):
    half = y.shape[0] // 2
    return y[:half] + y[half:]


def mm(x, w):
    return joined(jnp.dot(split(x), w, preferred_element_type=F32))


def dot_nt(x, w):
    return lax.dot_general(x, w, (((1,), (1,)), ((), ())), preferred_element_type=F32)


def mm_nt(x, w):
    return joined(dot_nt(split(x), w))


def iota(shape, dim):
    return lax.broadcasted_iota(jnp.int32, shape, dim)


def kernel(
    ng, nm,
    fcols, gcols, ccols,
    rhs, ftiles, fsends, fweights, fgroups,
    gtiles, gsends, gweights, ggroups, ctiles,
    sol_out, res_out,
    fhi, flo, ghi, glo, chi, clo,
    fscale, gscale, cscale,
    fsel, gsel, fagg, gagg,
    fext, gext, cext,
    fy, gy, cy,
    x0, x1, zed, img,
    fout, fin, gout, gin, gathered, cparts, sums_m, sums_g,
    fs_send, fs_recv, gs_send, gs_recv, ag_send, ag_recv, cg_send, cg_recv,
    sm_send, sm_recv, sg_send, sg_recv,
):
    grp, mem = lax.axis_index("grp"), lax.axis_index("mem")
    me = grp * nm + mem
    T = ftiles.shape[-1]
    nrhs = rhs.shape[0]
    nb0, nb1, nb2 = ftiles.shape[0], gtiles.shape[0], ctiles.shape[0]
    rows0, rows1, rows2 = nb0 * T, nb1 * T, nb2 * T
    halo0, halo1 = fsends.shape[1] // 2, gsends.shape[1] // 2
    h0, h1 = halo0 // T, halo1 // T
    own1 = rows0 // AGG1
    ob1 = own1 // T
    share = rows1 // AGG2
    place = lax.rem(grp * share, T)
    cblock = lax.div(grp * share, T)

    has_lower, has_upper = me > 0, me < ng * nm - 1
    low_id = jnp.maximum(me - 1, 0)
    up_id = jnp.minimum(me + 1, ng * nm - 1)
    lower = (lax.div(low_id, nm), lax.rem(low_id, nm))
    upper = (lax.div(up_id, nm), lax.rem(up_id, nm))
    g_lower, g_upper = grp > 0, grp < ng - 1
    lower_g = (jnp.maximum(grp - 1, 0), mem)
    upper_g = (jnp.minimum(grp + 1, ng - 1), mem)

    fin[...] = jnp.zeros_like(fin)
    gin[...] = jnp.zeros_like(gin)

    barrier = pltpu.get_barrier_semaphore()
    for d in range(1, nm):
        pl.semaphore_signal(barrier, inc=1, device_id=(grp, lax.rem(mem + d, nm)), device_id_type=MESH)
    for d in range(1, ng):
        pl.semaphore_signal(barrier, inc=1, device_id=(lax.rem(grp + d, ng), mem), device_id_type=MESH)

    @pl.when(has_lower)
    def _():
        pl.semaphore_signal(barrier, inc=1, device_id=lower, device_id_type=MESH)

    @pl.when(has_upper)
    def _():
        pl.semaphore_signal(barrier, inc=1, device_id=upper, device_id_type=MESH)

    eye = iota((T, T), 0) == iota((T, T), 1)

    def prepare(tiles, cols, hi, lo, scale, count):
        @pl.loop(0, count)
        def _(b):
            diagonal = jnp.zeros((1, T), F32)
            for k in range(3):
                t = tiles[b, k]
                d = jnp.sum(jnp.where(eye, t, 0.0), axis=0, keepdims=True)
                diagonal = diagonal + jnp.where(cols[b, k] == b, 1.0, 0.0) * d
                hi[b, :, k * T : (k + 1) * T] = high_part(t)
                lo[b, :, k * T : (k + 1) * T] = low_part(t)
            scale[:, pl.ds(pl.multiple_of(b * T, T), T)] = RELAXATION / diagonal

    prepare(ftiles, fcols, fhi, flo, fscale, nb0)

    def one_hot_rows(sel, lists, count):
        width = lists.shape[1]

        @pl.loop(0, count)
        def _(b):
            at = pl.multiple_of(b * T, T)
            sel[pl.ds(at, T), :] = jnp.where(iota((T, width), 0) + at == lists[...], 1.0, 0.0).astype(BF16)

    one_hot_rows(fsel, fsends, nb0)

    pl.semaphore_wait(
        barrier, nm - 1 + ng - 1 + has_lower.astype(jnp.int32) + has_upper.astype(jnp.int32)
    )

    def halo_pair(out, into, send, recv, h, slot, low_dev, up_dev):
        def copy(side, dev):
            return pltpu.make_async_remote_copy(
                src_ref=out.at[slot, pl.ds(side * h, h)],
                dst_ref=into.at[slot, pl.ds((1 - side) * h, h)],
                send_sem=send.at[slot, side],
                recv_sem=recv.at[slot, 1 - side],
                device_id=dev,
                device_id_type=MESH,
            )

        return copy(0, low_dev), copy(1, up_dev)

    def f_pair(slot):
        return halo_pair(fout, fin, fs_send, fs_recv, h0, slot, lower, upper)

    def g_pair(slot):
        return halo_pair(gout, gin, gs_send, gs_recv, h1, slot, lower_g, upper_g)

    def start(pair, low, up):
        @pl.when(low)
        def _():
            pair[0].start()

        @pl.when(up)
        def _():
            pair[1].start()

    def finish(pair, low, up):
        @pl.when(low)
        def _():
            pair[0].wait_send()
            pair[1].wait_recv()

        @pl.when(up)
        def _():
            pair[1].wait_send()
            pair[0].wait_recv()

    def fine_send(x, slot):
        picked = mm(x, fsel[...])
        for s in range(2 * h0):
            fout[slot, s] = picked[:, s * T : (s + 1) * T]
        start(f_pair(slot), has_lower, has_upper)

    def group_send(x, slot):
        picked = mm(x, gsel[...])
        for s in range(2 * h1):
            gout[slot, s] = picked[:, s * T : (s + 1) * T]
        start(g_pair(slot), g_lower, g_upper)

    def put_own(x, ext, count):
        parts = split(x)
        for b in range(count):
            ext[b] = parts[:, b * T : (b + 1) * T]

    def apply(ext, cols, hi, lo, y, count):
        step = 4 if count % 4 == 0 else (2 if count % 2 == 0 else 1)

        @pl.loop(0, count // step)
        def _(i):
            for j in range(step):
                b = i * step + j
                xs = jnp.concatenate([ext[cols[b, k]] for k in range(3)], axis=1)
                r = joined(dot_nt(xs, hi[b])) + dot_nt(xs[:nrhs], lo[b])
                y[:, pl.ds(pl.multiple_of(b * T, T), T)] = r

    def fine_apply(slot):
        finish(f_pair(slot), has_lower, has_upper)
        for s in range(2 * h0):
            fext[nb0 + s] = split(fin[slot, s])
        apply(fext, fcols, fhi, flo, fy, nb0)
        return fy[...]

    def group_apply(slot):
        finish(g_pair(slot), g_lower, g_upper)
        for s in range(2 * h1):
            gext[nb1 + s] = split(gin[slot, s])
        apply(gext, gcols, ghi, glo, gy, nb1)
        return gy[...]

    def spread_copies(buf, it, mine, size, send, recv, axis):
        n = nm if axis == "mem" else ng
        out = []
        for d in range(1, n):
            dev = (grp, lax.rem(mem + d, nm)) if axis == "mem" else (lax.rem(grp + d, ng), mem)
            ref = buf.at[it, pl.ds(mine * size, size)]
            out.append(
                pltpu.make_async_remote_copy(
                    src_ref=ref, dst_ref=ref,
                    send_sem=send.at[it, d - 1], recv_sem=recv.at[it, d - 1],
                    device_id=dev, device_id_type=MESH,
                )
            )
        return out

    def run(copies):
        for c in copies:
            c.start()
        for c in copies:
            c.wait()

    def reduced(quantities, it):
        lanes = iota((8, T), 1)
        packed = jnp.zeros((8, T), F32)
        groups = nrhs // 8
        nq = len(quantities)
        for q, (a, b) in enumerate(quantities):
            s = jnp.sum(a * b, axis=1, keepdims=True)
            for k in range(groups):
                packed = jnp.where(lanes == k * nq + q, s[8 * k : 8 * k + 8], packed)
        sums_m[it, mem] = packed
        run(spread_copies(sums_m, it, mem, 1, sm_send, sm_recv, "mem"))
        total = sums_m[it, 0]
        for m in range(1, nm):
            total = total + sums_m[it, m]
        sums_g[it, grp] = total
        run(spread_copies(sums_g, it, grp, 1, sg_send, sg_recv, "grp"))
        total = sums_g[it, 0]
        for g in range(1, ng):
            total = total + sums_g[it, g]
        return [
            jnp.concatenate([total[:, k * nq + q : k * nq + q + 1] for k in range(groups)], axis=0)
            for q in range(nq)
        ]

    res_out[...] = rhs[...]
    start_x = fscale[...] * rhs[...]
    fine_send(start_x, 0)
    put_own(start_x, fext, nb0)
    x0[...] = start_x

    fagg[...] = jnp.where(iota((own1, rows0), 0) == fgroups[...], 1.0, 0.0).astype(BF16)
    gagg[...] = jnp.where(iota((T, rows1), 0) == ggroups[...] + place, 1.0, 0.0).astype(BF16)
    prepare(gtiles, gcols, ghi, glo, gscale, nb1)
    prepare(ctiles, ccols, chi, clo, cscale, nb2)
    one_hot_rows(gsel, gsends, nb1)

    for it in range(ITERS):
        base, gbase = 3 * it, 2 * it
        left = res_out[...] - (fine_apply(base) if it == 0 else fy[...])
        lowered = mm_nt(left * fweights[...], fagg[...])
        for s in range(ob1):
            gathered[it, mem * ob1 + s] = lowered[:, s * T : (s + 1) * T]
        run(spread_copies(gathered, it, mem, ob1, ag_send, ag_recv, "mem"))
        b1 = jnp.concatenate([gathered[it, b] for b in range(nb1)], axis=1)
        first = gscale[...] * b1
        group_send(first, gbase)
        put_own(first, gext, nb1)
        left = b1 - group_apply(gbase)
        cparts[it, grp] = mm_nt(left * gweights[...], gagg[...])
        run(spread_copies(cparts, it, grp, 1, cg_send, cg_recv, "grp"))
        per = T // share
        blocks = []
        for c in range(nb2):
            total = cparts[it, c * per]
            for g in range(c * per + 1, (c + 1) * per):
                total = total + cparts[it, g]
            blocks.append(total)
        b2 = jnp.concatenate(blocks, axis=1)
        x2 = cscale[...] * b2
        put_own(x2, cext, nb2)
        apply(cext, ccols, chi, clo, cy, nb2)
        cy[...] = x2 + cscale[...] * (b2 - cy[...])
        raised = cy[:, pl.ds(pl.multiple_of(cblock * T, T), T)]
        x1v = first + gweights[...] * mm(raised, gagg[...])
        group_send(x1v, gbase + 1)
        put_own(x1v, gext, nb1)
        x1[...] = x1v + gscale[...] * (b1 - group_apply(gbase + 1))
        mine = x1[:, pl.ds(pl.multiple_of(mem * own1, T), own1)]
        x0v = x0[...] + fweights[...] * mm(mine, fagg[...])
        fine_send(x0v, base + 1)
        put_own(x0v, fext, nb0)
        z = x0v + fscale[...] * (res_out[...] - fine_apply(base + 1))
        fine_send(z, base + 2)
        put_own(z, fext, nb0)
        q = fine_apply(base + 2)
        if it == 0:
            zed[...] = z
            img[...] = q
            fine_send(fscale[...] * q, base + 3)
            energy, curvature = reduced([(res_out[...], z), (z, q)], it)
            step = energy / curvature
            sol_out[...] = step * zed[...]
            res = res_out[...] - step * img[...]
            res_out[...] = res
            x0v = fscale[...] * res
            x0[...] = x0v
            put_own(x0v, fext, nb0)
            finish(f_pair(base + 3), has_lower, has_upper)
            for s in range(2 * h0):
                fext[nb0 + s] = split(fin[0, s] - step * fin[base + 3, s])
            apply(fext, fcols, fhi, flo, fy, nb0)
        else:
            fresh, own, one, two = reduced(
                [(res_out[...], z), (z, q), (z, img[...]), (zed[...], q)], it
            )
            ratio = fresh / energy
            curvature = own + ratio * (one + two) + ratio * ratio * curvature
            step = fresh / curvature
            sol_out[...] = sol_out[...] + step * (z + ratio * zed[...])
            res_out[...] = res_out[...] - step * (q + ratio * img[...])


def shards(
    ng, nm,
    right_side, fine_tiles, fine_columns, fine_sends, fine_weights, fine_groups,
    group_tiles, group_columns, group_sends, group_weights, group_groups,
    coarse_tiles, coarse_columns,
):
    nrhs, rows0 = right_side.shape
    T = fine_tiles.shape[-1]
    nb0, nb1, nb2 = fine_tiles.shape[0], group_tiles.shape[0], coarse_tiles.shape[0]
    rows1, rows2 = nb1 * T, nb2 * T
    h0, h1 = fine_sends.shape[1] // T, group_sends.shape[1] // T
    own1 = rows0 // AGG1
    vm, dma = pltpu.VMEM, pltpu.SemaphoreType.DMA
    scratch = [
        vm((nb0, T, 3 * T), BF16), vm((nb0, T, 3 * T), BF16),
        vm((nb1, T, 3 * T), BF16), vm((nb1, T, 3 * T), BF16),
        vm((nb2, T, 3 * T), BF16), vm((nb2, T, 3 * T), BF16),
        vm((1, rows0), F32), vm((1, rows1), F32), vm((1, rows2), F32),
        vm((rows0, 2 * h0 * T), BF16), vm((rows1, 2 * h1 * T), BF16),
        vm((own1, rows0), BF16), vm((T, rows1), BF16),
        vm((nb0 + 2 * h0, 2 * nrhs, T), BF16),
        vm((nb1 + 2 * h1, 2 * nrhs, T), BF16),
        vm((nb2, 2 * nrhs, T), BF16),
        vm((nrhs, rows0), F32), vm((nrhs, rows1), F32), vm((nrhs, rows2), F32),
        vm((nrhs, rows0), F32), vm((nrhs, rows1), F32),
        vm((nrhs, rows0), F32), vm((nrhs, rows0), F32),
        vm((3 * ITERS, 2 * h0, nrhs, T), F32), vm((3 * ITERS, 2 * h0, nrhs, T), F32),
        vm((2 * ITERS, 2 * h1, nrhs, T), F32), vm((2 * ITERS, 2 * h1, nrhs, T), F32),
        vm((ITERS, nb1, nrhs, T), F32), vm((ITERS, ng, nrhs, T), F32),
        vm((ITERS, nm, 8, T), F32), vm((ITERS, ng, 8, T), F32),
        dma((3 * ITERS, 2)), dma((3 * ITERS, 2)),
        dma((2 * ITERS, 2)), dma((2 * ITERS, 2)),
        dma((ITERS, nm - 1)), dma((ITERS, nm - 1)),
        dma((ITERS, ng - 1)), dma((ITERS, ng - 1)),
        dma((ITERS, nm - 1)), dma((ITERS, nm - 1)),
        dma((ITERS, ng - 1)), dma((ITERS, ng - 1)),
    ]
    in_vm, in_sm = pl.BlockSpec(memory_space=pltpu.VMEM), pl.BlockSpec(memory_space=pltpu.SMEM)
    out = jax.ShapeDtypeStruct((nrhs, rows0), F32)
    return pl.pallas_call(
        functools.partial(kernel, ng, nm),
        out_shape=(out, out),
        in_specs=[in_sm] * 3 + [in_vm] * 10,
        out_specs=(in_vm, in_vm),
        scratch_shapes=scratch,
        compiler_params=pltpu.CompilerParams(
            collective_id=0, has_side_effects=True, vmem_limit_bytes=60 << 20
        ),
    )(
        fine_columns, group_columns, coarse_columns,
        right_side, fine_tiles, fine_sends.reshape(1, -1), fine_weights.reshape(1, -1),
        fine_groups.reshape(1, -1), group_tiles, group_sends.reshape(1, -1),
        group_weights.reshape(1, -1), group_groups.reshape(1, -1), coarse_tiles,
    )


def solution(mesh):
    both = ("grp", "mem")
    return jax.shard_map(
        functools.partial(shards, mesh.shape["grp"], mesh.shape["mem"]),
        mesh=mesh,
        in_specs=(
            P(None, both), P(both, None, None, None), P(both, None), P(both, None), P(both), P(both),
            P("grp", None, None, None), P("grp", None), P("grp", None), P("grp"), P("grp"),
            P(), P(),
        ),
        out_specs=(P(None, both), P(None, both)),
        check_vma=False,
    )
```

profile of v0, /device:TPU:0, one launch (start us, length us, event | category | flops | bytes accessed | tf_op | source)
XLA Modules:
  0.0 95.0 jit_solution(16966890850326569881)
XLA Ops:
  0.6 1.3 %copy.17 = s32[1,1,2,256]{3,1,2,0:T(1,128)} copy(s32[1,1,2,256]{3,2,1,0:T(2,128)} %bitcast.13) | data formatting | bytes 4096
  1.9 1.3 %copy.16.gcols = s32[8,3]{1,0:T(8,128)} copy(s32[8,3]{0,1:T(4,128)} %param.20) | data formatting | bytes 192 | tf_op args[7]
  3.2 1.4 %copy.15.fcols = s32[16,3]{1,0:T(8,128)} copy(s32[16,3]{0,1:T(4,128)} %param.15) | data formatting | bytes 384 | tf_op args[2]
  4.6 87.1 %shard_map.140 = (f32[32,2048]{1,0:T(8,128)}, f32[32,2048]{1,0:T(8,128)}) custom-call(s32[16,3]{1,0:T(8,128)} %copy.15.fcols, s32[8,3]{1,0:T(8,128)} %copy.16.gcols, s32[2,3]{1,0:T(2,128)} %ccols.1, f32[32,2048]{1,0:T(8,128)} %rhs.1, f32[16,3,128,128]{3,2,1,0:T(8,128)} %ftiles.1, s32[1,512]{1,0:T(1,128)} %bitcast.10, f32[1,2048]{1,0:T(1,128)} %bitcast.8, ...), custom_call_target="tpu_custom_call" | custom-call | tf_op jit(solution)/shard_map/pallas_call | solution.py:380
  91.7 1.7 %copy.20 = f32[32,2048]{1,0:T(8,128)} copy(f32[32,2048]{1,0:T(8,128)} %get-tuple-element.4) | data formatting | bytes 524288
  93.4 1.7 %copy.21 = f32[32,2048]{1,0:T(8,128)} copy(f32[32,2048]{1,0:T(8,128)} %get-tuple-element.5) | data formatting | bytes 524288
where the time goes:
time: 95.3 us; the launch traced here: 95 us
  Pallas kernels  87.1 us (91%)
  local copies, waits for them, and re-layouts  7.31 us (8%)
    pallas_call x1, Pallas kernels, shards(): pl.pallas_call(functools.partial(kernel, ng, nm), out_shape=(out, out), i...  87.1 us
    unnamed x5, local copies, waits for them, and re-layouts  7.31 us

commit v1 on v0

--- a/solution.py
+++ b/solution.py
@@ -50,19 +50,20 @@
 
 def kernel(
     ng, nm,
-    fcols, gcols, ccols,
+    fcols_ref, gcols_ref, ccols_ref,
     rhs, ftiles, fsends, fweights, fgroups,
-    gtiles, gsends, gweights, ggroups, ctiles,
+    gtiles_hbm, gsends, gweights, ggroups, ctiles_hbm,
     sol_out, res_out,
     fhi, flo, ghi, glo, chi, clo,
     fscale, gscale, cscale,
-    fsel, gsel, fagg, gagg,
+    gtiles, ctiles, fsel, gsel, fagg, gagg, gplain,
+    hp_out, hp_in, hp_hi, hp_lo,
     fext, gext, cext,
     fy, gy, cy,
     x0, x1, zed, img,
     fout, fin, gout, gin, gathered, cparts, sums_m, sums_g,
     fs_send, fs_recv, gs_send, gs_recv, ag_send, ag_recv, cg_send, cg_recv,
-    sm_send, sm_recv, sg_send, sg_recv,
+    sm_send, sm_recv, sg_send, sg_recv, hp_send, hp_recv, load_sem,
 ):
     grp, mem = lax.axis_index("grp"), lax.axis_index("mem")
     me = grp * nm + mem
@@ -70,7 +71,7 @@
     nrhs = rhs.shape[0]
     nb0, nb1, nb2 = ftiles.shape[0], gtiles.shape[0], ctiles.shape[0]
     rows0, rows1, rows2 = nb0 * T, nb1 * T, nb2 * T
-    halo0, halo1 = fsends.shape[1] // 2, gsends.shape[1] // 2
+    halo0, halo1 = fsends.shape[1], gsends.shape[1]
     h0, h1 = halo0 // T, halo1 // T
     own1 = rows0 // AGG1
     ob1 = own1 // T
@@ -87,8 +88,25 @@
     lower_g = (jnp.maximum(grp - 1, 0), mem)
     upper_g = (jnp.minimum(grp + 1, ng - 1), mem)
 
+    loads = [
+        pltpu.make_async_copy(gtiles_hbm, gtiles, load_sem.at[0]),
+        pltpu.make_async_copy(ctiles_hbm, ctiles, load_sem.at[1]),
+    ]
+    for load in loads:
+        load.start()
+
     fin[...] = jnp.zeros_like(fin)
+    hp_in[...] = jnp.zeros_like(hp_in)
     gin[...] = jnp.zeros_like(gin)
+
+    def fcols(k, b):
+        return fcols_ref[k, b]
+
+    def gcols(k, b):
+        return gcols_ref[k, b]
+
+    def ccols(k, b):
+        return ccols_ref[b, k]
 
     barrier = pltpu.get_barrier_semaphore()
     for d in range(1, nm):
@@ -113,7 +131,7 @@
             for k in range(3):
                 t = tiles[b, k]
                 d = jnp.sum(jnp.where(eye, t, 0.0), axis=0, keepdims=True)
-                diagonal = diagonal + jnp.where(cols[b, k] == b, 1.0, 0.0) * d
+                diagonal = diagonal + jnp.where(cols(k, b) == b, 1.0, 0.0) * d
                 hi[b, :, k * T : (k + 1) * T] = high_part(t)
                 lo[b, :, k * T : (k + 1) * T] = low_part(t)
             scale[:, pl.ds(pl.multiple_of(b * T, T), T)] = RELAXATION / diagonal
@@ -121,12 +139,13 @@
     prepare(ftiles, fcols, fhi, flo, fscale, nb0)
 
     def one_hot_rows(sel, lists, count):
-        width = lists.shape[1]
+        width = 2 * lists.shape[1]
+        row = jnp.concatenate([lists[0:1, :], lists[1:2, :]], axis=1)
 
         @pl.loop(0, count)
         def _(b):
             at = pl.multiple_of(b * T, T)
-            sel[pl.ds(at, T), :] = jnp.where(iota((T, width), 0) + at == lists[...], 1.0, 0.0).astype(BF16)
+            sel[pl.ds(at, T), :] = jnp.where(iota((T, width), 0) + at == row, 1.0, 0.0).astype(BF16)
 
     one_hot_rows(fsel, fsends, nb0)
 
@@ -190,30 +209,36 @@
         for b in range(count):
             ext[b] = parts[:, b * T : (b + 1) * T]
 
-    def apply(ext, cols, hi, lo, y, count):
+    def apply_own(ext, hi, lo, y, count):
         step = 4 if count % 4 == 0 else (2 if count % 2 == 0 else 1)
 
         @pl.loop(0, count // step)
         def _(i):
             for j in range(step):
                 b = i * step + j
-                xs = jnp.concatenate([ext[cols[b, k]] for k in range(3)], axis=1)
-                r = joined(dot_nt(xs, hi[b])) + dot_nt(xs[:nrhs], lo[b])
+                xs = ext[b]
+                r = joined(dot_nt(xs, hi[b, :, :T])) + dot_nt(xs[:nrhs], lo[b, :, :T])
                 y[:, pl.ds(pl.multiple_of(b * T, T), T)] = r
 
+    def apply_rest(ext, cols, hi, lo, y, count):
+        step = 4 if count % 4 == 0 else (2 if count % 2 == 0 else 1)
+
+        @pl.loop(0, count // step)
+        def _(i):
+            for j in range(step):
+                b = i * step + j
+                xs = jnp.concatenate([ext[cols(k, b)] for k in (1, 2)], axis=1)
+                r = joined(dot_nt(xs, hi[b, :, T:])) + dot_nt(xs[:nrhs], lo[b, :, T:])
+                at = pl.ds(pl.multiple_of(b * T, T), T)
+                y[:, at] = y[:, at] + r
+
     def fine_apply(slot):
+        apply_own(fext, fhi, flo, fy, nb0)
         finish(f_pair(slot), has_lower, has_upper)
         for s in range(2 * h0):
             fext[nb0 + s] = split(fin[slot, s])
-        apply(fext, fcols, fhi, flo, fy, nb0)
+        apply_rest(fext, fcols, fhi, flo, fy, nb0)
         return fy[...]
-
-    def group_apply(slot):
-        finish(g_pair(slot), g_lower, g_upper)
-        for s in range(2 * h1):
-            gext[nb1 + s] = split(gin[slot, s])
-        apply(gext, gcols, ghi, glo, gy, nb1)
-        return gy[...]
 
     def spread_copies(buf, it, mine, size, send, recv, axis):
         n = nm if axis == "mem" else ng
@@ -268,12 +293,52 @@
 
     fagg[...] = jnp.where(iota((own1, rows0), 0) == fgroups[...], 1.0, 0.0).astype(BF16)
     gagg[...] = jnp.where(iota((T, rows1), 0) == ggroups[...] + place, 1.0, 0.0).astype(BF16)
+    gplain[...] = jnp.where(iota((T, rows1), 0) == ggroups[...], 1.0, 0.0).astype(BF16)
+    one_hot_rows(gsel, gsends, nb1)
+
+    table = mm(gagg[...].astype(F32) * gweights[...], gsel[...])
+    for side in range(2):
+        hp_out[0, side] = table[:, side * halo1 : (side + 1) * halo1]
+
+    def hp_copy(side, dev):
+        return pltpu.make_async_remote_copy(
+            src_ref=hp_out.at[0, side], dst_ref=hp_in.at[0, 1 - side],
+            send_sem=hp_send.at[0, side], recv_sem=hp_recv.at[0, 1 - side],
+            device_id=dev, device_id_type=MESH,
+        )
+
+    hp_pair = (hp_copy(0, lower_g), hp_copy(1, upper_g))
+    start(hp_pair, g_lower, g_upper)
+    for load in loads:
+        load.wait()
     prepare(gtiles, gcols, ghi, glo, gscale, nb1)
     prepare(ctiles, ccols, chi, clo, cscale, nb2)
-    one_hot_rows(gsel, gsends, nb1)
+
+    per = T // share
+    piece = nrhs // per
+    lane = iota((piece, T), 1)
+
+    def packed_part(part):
+        out = part[:piece]
+        for k in range(1, per):
+            out = out + pltpu.roll(part[k * piece : (k + 1) * piece], k * share, 1)
+        return out
+
+    def coarse_block(it, c):
+        rows = []
+        for k in range(per):
+            total = jnp.zeros((piece, T), F32)
+            for r in range(per):
+                shift = ((r - k) * share) % T
+                got = cparts[it, c * per + r]
+                if shift:
+                    got = pltpu.roll(got, shift, 1)
+                total = jnp.where((lane >= r * share) & (lane < (r + 1) * share), got, total)
+            rows.append(total)
+        return jnp.concatenate(rows, axis=0)
 
     for it in range(ITERS):
-        base, gbase = 3 * it, 2 * it
+        base = 3 * it
         left = res_out[...] - (fine_apply(base) if it == 0 else fy[...])
         lowered = mm_nt(left * fweights[...], fagg[...])
         for s in range(ob1):
@@ -281,28 +346,43 @@
         run(spread_copies(gathered, it, mem, ob1, ag_send, ag_recv, "mem"))
         b1 = jnp.concatenate([gathered[it, b] for b in range(nb1)], axis=1)
         first = gscale[...] * b1
-        group_send(first, gbase)
+        group_send(first, it)
         put_own(first, gext, nb1)
-        left = b1 - group_apply(gbase)
-        cparts[it, grp] = mm_nt(left * gweights[...], gagg[...])
+        apply_own(gext, ghi, glo, gy, nb1)
+        finish(g_pair(it), g_lower, g_upper)
+        for s in range(2 * h1):
+            gext[nb1 + s] = split(gin[it, s])
+        apply_rest(gext, gcols, ghi, glo, gy, nb1)
+        left = b1 - gy[...]
+        cparts[it, grp] = packed_part(mm_nt(left * gweights[...], gplain[...]))
         run(spread_copies(cparts, it, grp, 1, cg_send, cg_recv, "grp"))
-        per = T // share
-        blocks = []
-        for c in range(nb2):
-            total = cparts[it, c * per]
-            for g in range(c * per + 1, (c + 1) * per):
-                total = total + cparts[it, g]
-            blocks.append(total)
-        b2 = jnp.concatenate(blocks, axis=1)
+        b2 = jnp.concatenate([coarse_block(it, c) for c in range(nb2)], axis=1)
         x2 = cscale[...] * b2
         put_own(x2, cext, nb2)
-        apply(cext, ccols, chi, clo, cy, nb2)
+        apply_own(cext, chi, clo, cy, nb2)
+        apply_rest(cext, ccols, chi, clo, cy, nb2)
         cy[...] = x2 + cscale[...] * (b2 - cy[...])
         raised = cy[:, pl.ds(pl.multiple_of(cblock * T, T), T)]
         x1v = first + gweights[...] * mm(raised, gagg[...])
-        group_send(x1v, gbase + 1)
         put_own(x1v, gext, nb1)
-        x1[...] = x1v + gscale[...] * (b1 - group_apply(gbase + 1))
+        if it == 0:
+            finish(hp_pair, g_lower, g_upper)
+            for side in range(2):
+                hp_hi[side] = high_part(hp_in[0, side])
+                hp_lo[side] = low_part(hp_in[0, side])
+        for side in range(2):
+            other = jnp.clip(grp + 2 * side - 1, 0, ng - 1)
+            oblock = lax.div(other * share, T)
+            far = split(cy[:, pl.ds(pl.multiple_of(oblock * T, T), T)])
+            lift = joined(jnp.dot(far, hp_hi[side], preferred_element_type=F32)) + jnp.dot(
+                far[:nrhs], hp_lo[side], preferred_element_type=F32
+            )
+            for s in range(h1):
+                at = side * h1 + s
+                gext[nb1 + at] = split(gin[it, at] + lift[:, s * T : (s + 1) * T])
+        apply_own(gext, ghi, glo, gy, nb1)
+        apply_rest(gext, gcols, ghi, glo, gy, nb1)
+        x1[...] = x1v + gscale[...] * (b1 - gy[...])
         mine = x1[:, pl.ds(pl.multiple_of(mem * own1, T), own1)]
         x0v = x0[...] + fweights[...] * mm(mine, fagg[...])
         fine_send(x0v, base + 1)
@@ -326,7 +406,8 @@
             finish(f_pair(base + 3), has_lower, has_upper)
             for s in range(2 * h0):
                 fext[nb0 + s] = split(fin[0, s] - step * fin[base + 3, s])
-            apply(fext, fcols, fhi, flo, fy, nb0)
+            apply_own(fext, fhi, flo, fy, nb0)
+            apply_rest(fext, fcols, fhi, flo, fy, nb0)
         else:
             fresh, own, one, two = reduced(
                 [(res_out[...], z), (z, q), (z, img[...]), (zed[...], q)], it
@@ -356,8 +437,11 @@
         vm((nb1, T, 3 * T), BF16), vm((nb1, T, 3 * T), BF16),
         vm((nb2, T, 3 * T), BF16), vm((nb2, T, 3 * T), BF16),
         vm((1, rows0), F32), vm((1, rows1), F32), vm((1, rows2), F32),
+        vm(group_tiles.shape, F32), vm(coarse_tiles.shape, F32),
         vm((rows0, 2 * h0 * T), BF16), vm((rows1, 2 * h1 * T), BF16),
-        vm((own1, rows0), BF16), vm((T, rows1), BF16),
+        vm((own1, rows0), BF16), vm((T, rows1), BF16), vm((T, rows1), BF16),
+        vm((1, 2, T, h1 * T), F32), vm((1, 2, T, h1 * T), F32),
+        vm((2, T, h1 * T), BF16), vm((2, T, h1 * T), BF16),
         vm((nb0 + 2 * h0, 2 * nrhs, T), BF16),
         vm((nb1 + 2 * h1, 2 * nrhs, T), BF16),
         vm((nb2, 2 * nrhs, T), BF16),
@@ -365,31 +449,33 @@
         vm((nrhs, rows0), F32), vm((nrhs, rows1), F32),
         vm((nrhs, rows0), F32), vm((nrhs, rows0), F32),
         vm((3 * ITERS, 2 * h0, nrhs, T), F32), vm((3 * ITERS, 2 * h0, nrhs, T), F32),
-        vm((2 * ITERS, 2 * h1, nrhs, T), F32), vm((2 * ITERS, 2 * h1, nrhs, T), F32),
-        vm((ITERS, nb1, nrhs, T), F32), vm((ITERS, ng, nrhs, T), F32),
+        vm((ITERS, 2 * h1, nrhs, T), F32), vm((ITERS, 2 * h1, nrhs, T), F32),
+        vm((ITERS, nb1, nrhs, T), F32), vm((ITERS, ng, nrhs * (rows1 // AGG2) // T, T), F32),
         vm((ITERS, nm, 8, T), F32), vm((ITERS, ng, 8, T), F32),
         dma((3 * ITERS, 2)), dma((3 * ITERS, 2)),
-        dma((2 * ITERS, 2)), dma((2 * ITERS, 2)),
+        dma((ITERS, 2)), dma((ITERS, 2)),
         dma((ITERS, nm - 1)), dma((ITERS, nm - 1)),
         dma((ITERS, ng - 1)), dma((ITERS, ng - 1)),
         dma((ITERS, nm - 1)), dma((ITERS, nm - 1)),
         dma((ITERS, ng - 1)), dma((ITERS, ng - 1)),
+        dma((1, 2)), dma((1, 2)), dma((2,)),
     ]
     in_vm, in_sm = pl.BlockSpec(memory_space=pltpu.VMEM), pl.BlockSpec(memory_space=pltpu.SMEM)
+    in_any = pl.BlockSpec(memory_space=pl.ANY)
     out = jax.ShapeDtypeStruct((nrhs, rows0), F32)
     return pl.pallas_call(
         functools.partial(kernel, ng, nm),
         out_shape=(out, out),
-        in_specs=[in_sm] * 3 + [in_vm] * 10,
+        in_specs=[in_sm] * 3 + [in_vm] * 5 + [in_any] + [in_vm] * 3 + [in_any],
         out_specs=(in_vm, in_vm),
         scratch_shapes=scratch,
         compiler_params=pltpu.CompilerParams(
             collective_id=0, has_side_effects=True, vmem_limit_bytes=60 << 20
         ),
     )(
-        fine_columns, group_columns, coarse_columns,
-        right_side, fine_tiles, fine_sends.reshape(1, -1), fine_weights.reshape(1, -1),
-        fine_groups.reshape(1, -1), group_tiles, group_sends.reshape(1, -1),
+        fine_columns.T, group_columns.T, coarse_columns,
+        right_side, fine_tiles, fine_sends, fine_weights.reshape(1, -1),
+        fine_groups.reshape(1, -1), group_tiles, group_sends,
         group_weights.reshape(1, -1), group_groups.reshape(1, -1), coarse_tiles,
     )
 

time: 95.3 us -> 81.3 us (0.85)
  Pallas kernels: 87.1 us -> 77.1 us
  local copies, waits for them, and re-layouts: 7.31 us -> 3.34 us
    pallas_call x1, Pallas kernels: 87.1 us -> 77.1 us  [shards(): pl.pallas_call(functools.partial(kernel, ng, nm), out_shape=(out, out), i...]
    unnamed x5 -> x2, local copies, waits for them, and re-layouts: 7.31 us -> 3.34 us
where the time goes in v1:
time: 81.3 us; the launch traced here: 81.1 us
  Pallas kernels  77.1 us (95%)
  local copies, waits for them, and re-layouts  3.34 us (4%)
    pallas_call x1, Pallas kernels, shards(): pl.pallas_call(functools.partial(kernel, ng, nm), out_shape=(out, out), i...  77.1 us
    unnamed x2, local copies, waits for them, and re-layouts  3.34 us

profile of v1, /device:TPU:0, one launch (start us, length us, event | category | flops | bytes accessed | tf_op | source)
XLA Modules:
  0.0 81.1 jit_solution(14266590673303576744)
XLA Ops:
  0.6 77.1 %shard_map.140 = (f32[32,2048]{1,0:T(8,128)}, f32[32,2048]{1,0:T(8,128)}) custom-call(s32[3,16]{1,0:T(4,128)} %bitcast.10, s32[3,8]{1,0:T(4,128)} %bitcast.11, s32[2,3]{1,0:T(2,128)} %ccols_ref.1, f32[32,2048]{1,0:T(8,128)} %rhs.1, f32[16,3,128,128]{3,2,1,0:T(8,128)} %ftiles.1, s32[2,256]{1,0:T(2,128)} %fsends.1, f32[1,2048]{1,0:T(1,128)} %bitcast.6, ...), custom_call_target="tpu_custom_call" | custom-call | tf_op jit(solution)/shard_map/pallas_call | solution.py:466
  77.8 1.7 %copy.17 = f32[32,2048]{1,0:T(8,128)} copy(f32[32,2048]{1,0:T(8,128)} %get-tuple-element.4) | data formatting | bytes 524288
  79.4 1.7 %copy.18 = f32[32,2048]{1,0:T(8,128)} copy(f32[32,2048]{1,0:T(8,128)} %get-tuple-element.5) | data formatting | bytes 524288

commit v2 on v1

--- a/solution.py
+++ b/solution.py
@@ -203,6 +203,7 @@
         for s in range(2 * h1):
             gout[slot, s] = picked[:, s * T : (s + 1) * T]
         start(g_pair(slot), g_lower, g_upper)
+        return picked
 
     def put_own(x, ext, count):
         parts = split(x)
@@ -298,20 +299,37 @@
 
     table = mm(gagg[...].astype(F32) * gweights[...], gsel[...])
     for side in range(2):
-        hp_out[0, side] = table[:, side * halo1 : (side + 1) * halo1]
+        hp_out[side, 0] = table[:, side * halo1 : (side + 1) * halo1]
+        hp_out[side, 1] = jnp.zeros((T, halo1), F32)
+    for load in loads:
+        load.wait()
+    prepare(gtiles, gcols, ghi, glo, gscale, nb1)
+
+    @pl.loop(0, nb1)
+    def _(b):
+        at = pl.ds(pl.multiple_of(b * T, T), T)
+        w = split(gplain[:share, at].astype(F32) * gweights[:, at])
+        r = joined(jnp.dot(w, ghi[b, :, T:], preferred_element_type=F32)) + jnp.dot(
+            w[:share], glo[b, :, T:], preferred_element_type=F32
+        )
+        for k in (1, 2):
+            for i in range(2 * h1):
+                side, s = i // h1, i % h1
+                hit = jnp.where(gcols(k, b) == nb1 + i, 1.0, 0.0)
+                span = slice(s * T, (s + 1) * T)
+                hp_out[side, 1, :share, span] = (
+                    hp_out[side, 1, :share, span] + hit * r[:, (k - 1) * T : k * T]
+                )
 
     def hp_copy(side, dev):
         return pltpu.make_async_remote_copy(
-            src_ref=hp_out.at[0, side], dst_ref=hp_in.at[0, 1 - side],
+            src_ref=hp_out.at[side], dst_ref=hp_in.at[1 - side],
             send_sem=hp_send.at[0, side], recv_sem=hp_recv.at[0, 1 - side],
             device_id=dev, device_id_type=MESH,
         )
 
     hp_pair = (hp_copy(0, lower_g), hp_copy(1, upper_g))
     start(hp_pair, g_lower, g_upper)
-    for load in loads:
-        load.wait()
-    prepare(gtiles, gcols, ghi, glo, gscale, nb1)
     prepare(ctiles, ccols, chi, clo, cscale, nb2)
 
     per = T // share
@@ -330,7 +348,12 @@
             total = jnp.zeros((piece, T), F32)
             for r in range(per):
                 shift = ((r - k) * share) % T
-                got = cparts[it, c * per + r]
+                g = c * per + r
+                got = cparts[it, g, :piece]
+                if g > 0:
+                    got = got + cparts[it, g - 1, 2 * piece :]
+                if g < ng - 1:
+                    got = got + cparts[it, g + 1, piece : 2 * piece]
                 if shift:
                     got = pltpu.roll(got, shift, 1)
                 total = jnp.where((lane >= r * share) & (lane < (r + 1) * share), got, total)
@@ -346,15 +369,24 @@
         run(spread_copies(gathered, it, mem, ob1, ag_send, ag_recv, "mem"))
         b1 = jnp.concatenate([gathered[it, b] for b in range(nb1)], axis=1)
         first = gscale[...] * b1
-        group_send(first, it)
+        picked = group_send(first, it)
         put_own(first, gext, nb1)
+        for s in range(2 * h1):
+            gext[nb1 + s] = jnp.zeros((2 * nrhs, T), BF16)
         apply_own(gext, ghi, glo, gy, nb1)
-        finish(g_pair(it), g_lower, g_upper)
-        for s in range(2 * h1):
-            gext[nb1 + s] = split(gin[it, s])
         apply_rest(gext, gcols, ghi, glo, gy, nb1)
         left = b1 - gy[...]
-        cparts[it, grp] = packed_part(mm_nt(left * gweights[...], gplain[...]))
+        cparts[it, grp, :piece] = packed_part(mm_nt(left * gweights[...], gplain[...]))
+        if it == 0:
+            finish(hp_pair, g_lower, g_upper)
+            for side in range(2):
+                for which in range(2):
+                    hp_hi[side, which] = high_part(hp_in[side, which])
+                    hp_lo[side, which] = low_part(hp_in[side, which])
+        for side in range(2):
+            given = split(picked[:, side * halo1 : (side + 1) * halo1])
+            felt = joined(dot_nt(given, hp_hi[side, 1])) + dot_nt(given[:nrhs], hp_lo[side, 1])
+            cparts[it, grp, (side + 1) * piece : (side + 2) * piece] = packed_part(-felt)
         run(spread_copies(cparts, it, grp, 1, cg_send, cg_recv, "grp"))
         b2 = jnp.concatenate([coarse_block(it, c) for c in range(nb2)], axis=1)
         x2 = cscale[...] * b2
@@ -365,17 +397,13 @@
         raised = cy[:, pl.ds(pl.multiple_of(cblock * T, T), T)]
         x1v = first + gweights[...] * mm(raised, gagg[...])
         put_own(x1v, gext, nb1)
-        if it == 0:
-            finish(hp_pair, g_lower, g_upper)
-            for side in range(2):
-                hp_hi[side] = high_part(hp_in[0, side])
-                hp_lo[side] = low_part(hp_in[0, side])
+        finish(g_pair(it), g_lower, g_upper)
         for side in range(2):
             other = jnp.clip(grp + 2 * side - 1, 0, ng - 1)
             oblock = lax.div(other * share, T)
             far = split(cy[:, pl.ds(pl.multiple_of(oblock * T, T), T)])
-            lift = joined(jnp.dot(far, hp_hi[side], preferred_element_type=F32)) + jnp.dot(
-                far[:nrhs], hp_lo[side], preferred_element_type=F32
+            lift = joined(jnp.dot(far, hp_hi[side, 0], preferred_element_type=F32)) + jnp.dot(
+                far[:nrhs], hp_lo[side, 0], preferred_element_type=F32
             )
             for s in range(h1):
                 at = side * h1 + s
@@ -440,8 +468,8 @@
         vm(group_tiles.shape, F32), vm(coarse_tiles.shape, F32),
         vm((rows0, 2 * h0 * T), BF16), vm((rows1, 2 * h1 * T), BF16),
         vm((own1, rows0), BF16), vm((T, rows1), BF16), vm((T, rows1), BF16),
-        vm((1, 2, T, h1 * T), F32), vm((1, 2, T, h1 * T), F32),
-        vm((2, T, h1 * T), BF16), vm((2, T, h1 * T), BF16),
+        vm((2, 2, T, h1 * T), F32), vm((2, 2, T, h1 * T), F32),
+        vm((2, 2, T, h1 * T), BF16), vm((2, 2, T, h1 * T), BF16),
         vm((nb0 + 2 * h0, 2 * nrhs, T), BF16),
         vm((nb1 + 2 * h1, 2 * nrhs, T), BF16),
         vm((nb2, 2 * nrhs, T), BF16),
@@ -450,7 +478,7 @@
         vm((nrhs, rows0), F32), vm((nrhs, rows0), F32),
         vm((3 * ITERS, 2 * h0, nrhs, T), F32), vm((3 * ITERS, 2 * h0, nrhs, T), F32),
         vm((ITERS, 2 * h1, nrhs, T), F32), vm((ITERS, 2 * h1, nrhs, T), F32),
-        vm((ITERS, nb1, nrhs, T), F32), vm((ITERS, ng, nrhs * (rows1 // AGG2) // T, T), F32),
+        vm((ITERS, nb1, nrhs, T), F32), vm((ITERS, ng, 3 * nrhs * (rows1 // AGG2) // T, T), F32),
         vm((ITERS, nm, 8, T), F32), vm((ITERS, ng, 8, T), F32),
         dma((3 * ITERS, 2)), dma((3 * ITERS, 2)),
         dma((ITERS, 2)), dma((ITERS, 2)),

time: 81.3 us -> 80.1 us (0.985)
  Pallas kernels: 77.1 us -> 75.9 us
    pallas_call x1, Pallas kernels: 77.1 us -> 75.9 us  [shards(): pl.pallas_call(functools.partial(kernel, ng, nm), out_shape=(out, out), i...]
where the time goes in v2:
time: 80.1 us; the launch traced here: 79.9 us
  Pallas kernels  75.9 us (95%)
  local copies, waits for them, and re-layouts  3.34 us (4%)
    pallas_call x1, Pallas kernels, shards(): pl.pallas_call(functools.partial(kernel, ng, nm), out_shape=(out, out), i...  75.9 us
    unnamed x2, local copies, waits for them, and re-layouts  3.34 us

profile of v2, /device:TPU:0, one launch (start us, length us, event | category | flops | bytes accessed | tf_op | source)
XLA Modules:
  0.0 79.9 jit_solution(18089012438251158843)
XLA Ops:
  0.6 75.9 %shard_map.140 = (f32[32,2048]{1,0:T(8,128)}, f32[32,2048]{1,0:T(8,128)}) custom-call(s32[3,16]{1,0:T(4,128)} %bitcast.10, s32[3,8]{1,0:T(4,128)} %bitcast.11, s32[2,3]{1,0:T(2,128)} %ccols_ref.1, f32[32,2048]{1,0:T(8,128)} %rhs.1, f32[16,3,128,128]{3,2,1,0:T(8,128)} %ftiles.1, s32[2,256]{1,0:T(2,128)} %fsends.1, f32[1,2048]{1,0:T(1,128)} %bitcast.6, ...), custom_call_target="tpu_custom_call" | custom-call | tf_op jit(solution)/shard_map/pallas_call | solution.py:494
  76.6 1.7 %copy.17 = f32[32,2048]{1,0:T(8,128)} copy(f32[32,2048]{1,0:T(8,128)} %get-tuple-element.4) | data formatting | bytes 524288
  78.2 1.7 %copy.18 = f32[32,2048]{1,0:T(8,128)} copy(f32[32,2048]{1,0:T(8,128)} %get-tuple-element.5) | data formatting | bytes 524288

commit v3 on v2

--- a/solution.py
+++ b/solution.py
@@ -53,7 +53,7 @@
     fcols_ref, gcols_ref, ccols_ref,
     rhs, ftiles, fsends, fweights, fgroups,
     gtiles_hbm, gsends, gweights, ggroups, ctiles_hbm,
-    sol_out, res_out,
+    both_out,
     fhi, flo, ghi, glo, chi, clo,
     fscale, gscale, cscale,
     gtiles, ctiles, fsel, gsel, fagg, gagg, gplain,
@@ -65,6 +65,7 @@
     fs_send, fs_recv, gs_send, gs_recv, ag_send, ag_recv, cg_send, cg_recv,
     sm_send, sm_recv, sg_send, sg_recv, hp_send, hp_recv, load_sem,
 ):
+    sol_out, res_out = both_out.at[0], both_out.at[1]
     grp, mem = lax.axis_index("grp"), lax.axis_index("mem")
     me = grp * nm + mem
     T = ftiles.shape[-1]
@@ -211,7 +212,7 @@
             ext[b] = parts[:, b * T : (b + 1) * T]
 
     def apply_own(ext, hi, lo, y, count):
-        step = 4 if count % 4 == 0 else (2 if count % 2 == 0 else 1)
+        step = next(n for n in (8, 4, 2, 1) if count % n == 0)
 
         @pl.loop(0, count // step)
         def _(i):
@@ -222,7 +223,7 @@
                 y[:, pl.ds(pl.multiple_of(b * T, T), T)] = r
 
     def apply_rest(ext, cols, hi, lo, y, count):
-        step = 4 if count % 4 == 0 else (2 if count % 2 == 0 else 1)
+        step = next(n for n in (8, 4, 2, 1) if count % n == 0)
 
         @pl.loop(0, count // step)
         def _(i):
@@ -262,7 +263,7 @@
         for c in copies:
             c.wait()
 
-    def reduced(quantities, it):
+    def reduced(quantities, it, beside=None):
         lanes = iota((8, T), 1)
         packed = jnp.zeros((8, T), F32)
         groups = nrhs // 8
@@ -272,7 +273,13 @@
             for k in range(groups):
                 packed = jnp.where(lanes == k * nq + q, s[8 * k : 8 * k + 8], packed)
         sums_m[it, mem] = packed
-        run(spread_copies(sums_m, it, mem, 1, sm_send, sm_recv, "mem"))
+        copies = spread_copies(sums_m, it, mem, 1, sm_send, sm_recv, "mem")
+        for c in copies:
+            c.start()
+        if beside is not None:
+            beside()
+        for c in copies:
+            c.wait()
         total = sums_m[it, 0]
         for m in range(1, nm):
             total = total + sums_m[it, m]
@@ -422,8 +429,10 @@
         if it == 0:
             zed[...] = z
             img[...] = q
-            fine_send(fscale[...] * q, base + 3)
-            energy, curvature = reduced([(res_out[...], z), (z, q)], it)
+            energy, curvature = reduced(
+                [(res_out[...], z), (z, q)], it,
+                lambda: fine_send(fscale[...] * img[...], base + 3),
+            )
             step = energy / curvature
             sol_out[...] = step * zed[...]
             res = res_out[...] - step * img[...]
@@ -445,6 +454,11 @@
             step = fresh / curvature
             sol_out[...] = sol_out[...] + step * (z + ratio * zed[...])
             res_out[...] = res_out[...] - step * (q + ratio * img[...])
+
+
+def hand_over(both, sol, res):
+    sol[...] = both[0]
+    res[...] = both[1]
 
 
 def shards(
@@ -491,11 +505,11 @@
     in_vm, in_sm = pl.BlockSpec(memory_space=pltpu.VMEM), pl.BlockSpec(memory_space=pltpu.SMEM)
     in_any = pl.BlockSpec(memory_space=pl.ANY)
     out = jax.ShapeDtypeStruct((nrhs, rows0), F32)
-    return pl.pallas_call(
+    both = pl.pallas_call(
         functools.partial(kernel, ng, nm),
-        out_shape=(out, out),
+        out_shape=jax.ShapeDtypeStruct((2, nrhs, rows0), F32),
         in_specs=[in_sm] * 3 + [in_vm] * 5 + [in_any] + [in_vm] * 3 + [in_any],
-        out_specs=(in_vm, in_vm),
+        out_specs=in_vm,
         scratch_shapes=scratch,
         compiler_params=pltpu.CompilerParams(
             collective_id=0, has_side_effects=True, vmem_limit_bytes=60 << 20
@@ -506,6 +520,9 @@
         fine_groups.reshape(1, -1), group_tiles, group_sends,
         group_weights.reshape(1, -1), group_groups.reshape(1, -1), coarse_tiles,
     )
+    return pl.pallas_call(
+        hand_over, out_shape=(out, out), in_specs=[in_vm], out_specs=(in_vm, in_vm)
+    )(both)
 
 
 def solution(mesh):

time: 80.1 us -> 74.8 us (0.934)
  local copies, waits for them, and re-layouts: 3.34 us -> 0 us
  Pallas kernels: 75.9 us -> 74 us
    unnamed x2 -> x0, local copies, waits for them, and re-layouts: 3.34 us -> none
    pallas_call x1 -> x2, Pallas kernels: 75.9 us -> 74 us  [the longest x1 72.2 us: shards(): pl.pallas_call(functools.partial(kernel, ng, nm), out_shape=jax.ShapeDtyp...]
where the time goes in v3:
time: 74.8 us; the launch traced here: 74.7 us
  Pallas kernels  74 us (99%)
    pallas_call x1, Pallas kernels, shards(): pl.pallas_call(functools.partial(kernel, ng, nm), out_shape=jax.ShapeDtyp...  72.2 us
    pallas_call x1, Pallas kernels, shards(): pl.pallas_call(hand_over, out_shape=(out, out), in_specs=[in_vm], out_spe...  1.85 us

profile of v3, /device:TPU:0, one launch (start us, length us, event | category | flops | bytes accessed | tf_op | source)
XLA Modules:
  0.0 74.7 jit_solution(2201310594988041839)
XLA Ops:
  0.6 72.2 %shard_map.140.both = f32[2,32,2048]{2,1,0:T(8,128)} custom-call(s32[3,16]{1,0:T(4,128)} %bitcast.10, s32[3,8]{1,0:T(4,128)} %bitcast.11, s32[2,3]{1,0:T(2,128)} %ccols_ref.1, f32[32,2048]{1,0:T(8,128)} %rhs.1, f32[16,3,128,128]{3,2,1,0:T(8,128)} %ftiles.1, s32[2,256]{1,0:T(2,128)} %fsends.1, f32[1,2048]{1,0:T(1,128)} %bitcast.6, s32[1,2048]{1,0:T(1,128)} %bitcast.7, ...), custom_call_target="tpu_custom_call" | custom-call | tf_op jit(solution)/shard_map/pallas_call | solution.py:508
  72.8 1.8 %shard_map.141 = (f32[32,2048]{1,0:T(8,128)}, f32[32,2048]{1,0:T(8,128)}) custom-call(f32[2,32,2048]{2,1,0:T(8,128)} %shard_map.140.both), custom_call_target="tpu_custom_call" | custom-call | tf_op jit(solution)/shard_map/pallas_call | solution.py:523
